TPU v7x, 512 devices: a whole 4x8x8 slice. The times are simulated.
512 devices in a mesh: items: 32 (over x, y), cents: 16 (over z, core).
Axes of the slice: x: 4, y: 8, z: 8, core: 2. Of those that a mesh axis runs over, the one named last changes fastest.
Arguments:
- embeddings: bfloat16 [61440, 1024], P('items')
- counts: int32 [32], P('items'), may hold values from 1152 to 1920, as said below
- centroids: bfloat16 [2048, 1024], P('cents')
Outputs:
- final_centroids: bfloat16 [2048, 1024], P('cents')
Inputs may be any that keep to these rules, and one draw needn't show every extreme that they name: The counts of replicas 0 to i-1 sum to 1536 * i plus an offset of at most 192 in either direction, reached both ways in every draw; all counts sum to 49152. Rows of a buffer past its count carry no data.
All inputs are finite; a program needn't handle non-finite values.
Results may differ from a plain program's by a relative error of at most 0.0112.
Values may be sent and summed in bfloat16 or wider, within the bound.
No kernel may reach another device: no remote copies, remote signals or barrier semaphores. Data moves between devices by JAX's collectives and lax.ppermute only.
A program may use at most 64 MiB of HBM per device.

v0:
```python
import jax
import jax.numpy as jnp
from jax import lax
from jax.sharding import PartitionSpec as P

D = 1024
ROWS_DEV = 1536
ITERS = 2
SPILL = 192
prior_count = 2.0


def prefix(part, axis, combine, identity):
    place = lax.axis_index(axis)
    gathered = lax.all_gather(part, axis)
    state = jnp.zeros_like(part) + jnp.asarray(identity, part.dtype)

    def one(hop, state):
        return combine(state, lax.dynamic_index_in_dim(gathered, hop, 0, False))

    return lax.fori_loop(0, place, one, state)


def with_halo(block, sides, width):
    for axis, dim in sides:
        count = lax.axis_size(axis)
        forward = [(i, i + 1) for i in range(count - 1)]
        backward = [(target, source) for source, target in forward]
        low = lax.ppermute(
            lax.slice_in_dim(block, block.shape[dim] - width, None, axis=dim), axis, forward
        )
        high = lax.ppermute(lax.slice_in_dim(block, 0, width, axis=dim), axis, backward)
        block = jnp.concatenate([low, block, high], axis=dim)
    return block


def add_counts(earlier, later):
    return earlier + later


def settle_rows(embeddings, counts):
    capacity = embeddings.shape[0]
    own_count = counts[0]
    position = lax.axis_index("items")
    before = prefix(counts, "items", add_counts, jnp.zeros((1,), jnp.int32))[0]
    excess_below = before - position * ROWS_DEV
    excess_here = excess_below + own_count - ROWS_DEV
    from_below = jnp.maximum(excess_below, 0)
    sent_down = jnp.maximum(-excess_below, 0)
    from_above = jnp.maximum(-excess_here, 0)
    tail_rows = lax.dynamic_slice_in_dim(embeddings, own_count - SPILL, SPILL, 0)
    edge_rows = jnp.concatenate([embeddings[:SPILL], tail_rows], axis=0)
    extended = with_halo(edge_rows, (("items", 0),), SPILL)
    lower_rows = extended[:SPILL]
    upper_rows = extended[3 * SPILL :]
    joined = jnp.concatenate([lower_rows, embeddings, upper_rows], axis=0)
    slot_ids = jnp.arange(ROWS_DEV, dtype=jnp.int32)
    kept_rows = ROWS_DEV - from_below - from_above
    source = jnp.where(
        slot_ids < from_below,
        SPILL - from_below + slot_ids,
        jnp.where(
            slot_ids < from_below + kept_rows,
            SPILL + sent_down + slot_ids - from_below,
            SPILL + capacity + slot_ids - from_below - kept_rows,
        ),
    )
    return jnp.take(joined, source, axis=0)


def body(embeddings, counts, centroids):
    settled = settle_rows(embeddings, counts)
    scale = D ** (-0.5)
    current = centroids
    for step in range(ITERS):
        cent_f = current.astype(jnp.float32)
        norms = jnp.sum(cent_f * cent_f, axis=1)
        dots = lax.dot_general(
            settled, current, (((1,), (1,)), ((), ())), preferred_element_type=jnp.float32
        )
        score = (2.0 * dots - norms[None, :]) * scale
        top = lax.pmax(jnp.max(score, axis=1), "cents")
        expo = jnp.exp(score - top[:, None])
        total = lax.psum(jnp.sum(expo, axis=1), "cents")
        resp = (expo / total[:, None]).astype(jnp.bfloat16)
        mass_here = jnp.sum(resp.astype(jnp.float32), axis=0)
        moment_here = lax.dot_general(
            resp, settled, (((0,), (0,)), ((), ())), preferred_element_type=jnp.float32
        )
        moment, mass = lax.psum((moment_here, mass_here), "items")
        current = ((moment + prior_count * cent_f) / (mass[:, None] + prior_count)).astype(
            jnp.bfloat16
        )
    return current


def solution(mesh):
    in_specs = (P("items", None), P("items"), P("cents", None))
    out_specs = P("cents", None)
    return jax.shard_map(body, mesh=mesh, in_specs=in_specs, out_specs=out_specs, check_vma=False)
```

profile of v0, /device:TPU:64, one launch (start us, length us, event | category | flops | bytes accessed | tf_op | source)
XLA Modules:
  0.0 527.3 jit_solution(12058598038848635442)
XLA Ops:
  6.5 0.0 all-reduce.4.cloned.1.call-start
  7.2 1.3 constant_dynamic-slice_fusion.1
  8.5 3.5 collective-permute-start
  12.0 1.3 collective-permute-start.1
  13.3 1.3 dynamic-slice
  14.6 0.7 dynamic-update-slice
  15.4 25.5 %all-reduce = s32[32]{0:T(128)S(1)} all-reduce(s32[32]{0:T(128)S(1)} %dynamic-update-slice), channel_id=2, replica_groups=mesh['items'=32,'cents'=16] {'items'}, use_global_device_ids=true, to_apply=%add | all-reduce | flops 32 | bytes 256
  40.9 1.1 fusion.6
  42.0 0.0 collective-permute-done
  42.0 0.0 collective-permute-done.1
  42.0 3.9 pad_maximum_fusion
  46.0 0.0 copy-start
  46.0 10.8 %gather_fusion = bf16[1536,1024]{1,0:T(8,128)(2,1)} fusion(bf16[2304,1024]{1,0:T(8,128)(2,1)} %pad_maximum_fusion, s32[2048]{0:T(1024)S(1)} %pad_clamp_fusion), kind=kCustom, calls=%fused_computation | custom fusion | bytes 6297600 | tf_op jit(solution)/shard_map/jit(_take)/gather | solution.py:68
  56.7 0.0 copy-done
  56.7 3.2 fusion.18
  59.9 25.9 %pmax.14 = f32[1536]{0:T(1024)S(1)} all-reduce(f32[1536]{0:T(1024)S(1)} %get-tuple-element.45), channel_id=1, replica_groups=mesh['items'=32,'cents'=16] {'cents'}, use_global_device_ids=true, to_apply=%region_4.5 | all-reduce | flops 1536 | bytes 12288 | tf_op jit(solution)/shard_map/pmax | solution.py:82
  85.8 0.1 fusion.4
  85.9 24.4 %psum.42 = f32[1536]{0:T(1024)S(1)} all-reduce(f32[1536]{0:T(1024)S(1)} %fusion.4), channel_id=1, replica_groups=mesh['items'=32,'cents'=16] {'cents'}, use_global_device_ids=true, to_apply=%region_6.7 | all-reduce | flops 1536 | bytes 12288 | tf_op jit(solution)/shard_map/psum | solution.py:84
  110.3 0.2 convert_reduce_fusion.1
  110.6 3.4 fusion.16
  114.0 0.0 all-reduce.4.cloned.1.call-update
  114.0 0.0 all-reduce.6.cloned.1.call-start
  114.1 107.7 %psum.44 = f32[128]{0:T(128)S(1)} all-reduce(f32[128]{0:T(128)S(1)} %get-tuple-element.41), channel_id=1, replica_groups=mesh['items'=32,'cents'=16] {'items'}, use_global_device_ids=true, to_apply=%region_9.10 | all-reduce | flops 128 | bytes 1024 | tf_op jit(solution)/shard_map/psum | solution.py:90
  221.8 84.7 %all-reduce.4.cloned.1.call-done = f32[128,1024]{1,0:T(8,128)} async-done(((f32[128,1024]{1,0:T(8,128)}), f32[128,1024]{1,0:T(8,128)}) %all-reduce.4.cloned.1.call-update) | async-done | bytes 524304 | tf_op jit(solution)/shard_map/psum | solution.py:90
  306.5 1.3 fusion.10
  307.7 3.2 fusion.19
  310.9 21.5 %pmax.15 = f32[1536]{0:T(1024)S(1)} all-reduce(f32[1536]{0:T(1024)S(1)} %get-tuple-element.47), channel_id=1, replica_groups=mesh['items'=32,'cents'=16] {'cents'}, use_global_device_ids=true, to_apply=%region_12.13 | all-reduce | flops 1536 | bytes 12288 | tf_op jit(solution)/shard_map/pmax | solution.py:82
  332.4 0.1 fusion.5
  332.6 24.4 %psum.45 = f32[1536]{0:T(1024)S(1)} all-reduce(f32[1536]{0:T(1024)S(1)} %fusion.5), channel_id=1, replica_groups=mesh['items'=32,'cents'=16] {'cents'}, use_global_device_ids=true, to_apply=%region_14.15 | all-reduce | flops 1536 | bytes 12288 | tf_op jit(solution)/shard_map/psum | solution.py:84
  357.0 0.2 convert_reduce_fusion
  357.2 3.4 fusion.15
  360.6 0.0 all-reduce.6.cloned.1.call-update
  360.6 72.6 %psum.47 = f32[128]{0:T(128)S(1)} all-reduce(f32[128]{0:T(128)S(1)} %get-tuple-element.37), channel_id=1, replica_groups=mesh['items'=32,'cents'=16] {'items'}, use_global_device_ids=true, to_apply=%region_17.18 | all-reduce | flops 128 | bytes 1024 | tf_op jit(solution)/shard_map/psum | solution.py:90
  433.3 85.3 %all-reduce.6.cloned.1.call-done = f32[128,1024]{1,0:T(8,128)} async-done(((f32[128,1024]{1,0:T(8,128)}), f32[128,1024]{1,0:T(8,128)}) %all-reduce.6.cloned.1.call-update) | async-done | bytes 524304 | tf_op jit(solution)/shard_map/psum | solution.py:90
  518.6 1.9 fusion.13
  (7 shorter events, 0.1 us)
Async XLA Ops:
  6.5 300.0 %all-reduce.4.cloned.1.call-start = ((), (), s32[]{:S(2)}) async-start(), calls=%async_computation | async-start | bytes 1048576 | tf_op jit(solution)/shard_map/psum | solution.py:90
  8.5 33.6 %collective-permute-start = (bf16[192,1024]{1,0:T(8,128)(2,1)S(1)}, bf16[192,1024]{1,0:T(8,128)(2,1)S(1)}, u32[]{:S(2)}, u32[]{:S(2)}) collective-permute-start(bf16[192,1024]{1,0:T(8,128)(2,1)S(1)} %get-tuple-element.43), channel_id=1, source_target_pairs={{0,16},{16,32},{32,48},{48,64},{64,80},{80,96},{96,112},{112,128},... | collective-permute-start | bytes 1179656 | tf_op jit(solution)/shard_map/ppermute | solution.py:29
  12.0 30.1 %collective-permute-start.1 = (bf16[192,1024]{1,0:T(8,128)(2,1)S(1)}, bf16[192,1024]{1,0:T(8,128)(2,1)S(1)}, u32[]{:S(2)}, u32[]{:S(2)}) collective-permute-start(bf16[192,1024]{1,0:T(8,128)(2,1)S(1)} %get-tuple-element.44), channel_id=1, source_target_pairs={{16,0},{32,16},{48,32},{64,48},{80,64},{96,80},{112,96},{128,112},... | collective-permute-start | bytes 1179656 | tf_op jit(solution)/shard_map/ppermute | solution.py:32
  46.0 10.8 %copy-start = (bf16[128,1024]{1,0:T(8,128)(2,1)S(1)}, bf16[128,1024]{1,0:T(8,128)(2,1)}, u32[]{:S(2)}) copy-start(bf16[128,1024]{1,0:T(8,128)(2,1)} %param.7) | copy-start | bytes 786436
  114.0 404.6 %all-reduce.6.cloned.1.call-start = ((), (), s32[]{:S(2)}) async-start(), calls=%async_computation.1 | async-start | bytes 1048576 | tf_op jit(solution)/shard_map/psum | solution.py:90
Sparse Core Ops, SparseCore 0:
  114.2 192.2 all-reduce.3
  360.8 157.7 all-reduce.5
where the time goes:
time: 528 us; the launch traced here: 527 us
  blocking collectives  302 us (57%)
  waiting for transfers between devices  170 us (32%)
  between operations  14.2 us (3%)
  local copies, waits for them, and re-layouts  14.1 us (3%)
  matrix products  13.2 us (2%)
  other arithmetic  8.94 us (2%)
    psum x2, blocking collectives, body(): moment, mass = lax.psum((moment_here, mass_here), 'items')  180 us
    psum x2, waiting for transfers between devices, body(): moment, mass = lax.psum((moment_here, mass_here), 'items')  170 us
    psum x2, blocking collectives, body(): total = lax.psum(jnp.sum(expo, axis=1), 'cents')  48.8 us
    pmax x2, blocking collectives, body(): top = lax.pmax(jnp.max(score, axis=1), 'cents')  47.4 us
    unnamed x1, blocking collectives  25.5 us
    gather x1, local copies, waits for them, and re-layouts, settle_rows(): return jnp.take(joined, source, axis=0)  10.8 us
  transfers between devices with their start and end apart: 4, of which 2 were waited for; matrix products, arithmetic and copies ran while one was open for 1% of the time, Pallas kernels for 0%

commit v1 on v0

--- a/solution.py
+++ b/solution.py
@@ -81,7 +81,7 @@
         score = (2.0 * dots - norms[None, :]) * scale
         top = lax.pmax(jnp.max(score, axis=1), "cents")
         expo = jnp.exp(score - top[:, None])
-        total = lax.psum(jnp.sum(expo, axis=1), "cents")
+        total = jnp.sum(lax.all_gather(jnp.sum(expo, axis=1), "cents"), axis=0)
         resp = (expo / total[:, None]).astype(jnp.bfloat16)
         mass_here = jnp.sum(resp.astype(jnp.float32), axis=0)
         moment_here = lax.dot_general(

time: 528 us -> 510 us (0.966)
  blocking collectives: 302 us -> 290 us
  waiting for transfers between devices: 170 us -> 164 us
    psum x2 -> x0, blocking collectives: 48.8 us -> none  [body(): total = lax.psum(jnp.sum(expo, axis=1), 'cents')]
    all_gather x0 -> x2, blocking collectives: none -> 36.5 us  [body(): total = jnp.sum(lax.all_gather(jnp.sum(expo, axis=1), 'cents'), axis=0)]
    psum x2, waiting for transfers between devices: 170 us -> 164 us  [body(): moment, mass = lax.psum((moment_here, mass_here), 'items')]
where the time goes in v1:
time: 510 us; the launch traced here: 509 us
  blocking collectives  290 us (57%)
  waiting for transfers between devices  164 us (32%)
  between operations  14.2 us (3%)
  local copies, waits for them, and re-layouts  14.1 us (3%)
  matrix products  13.2 us (3%)
  other arithmetic  9.08 us (2%)
    psum x2, blocking collectives, body(): moment, mass = lax.psum((moment_here, mass_here), 'items')  180 us
    psum x2, waiting for transfers between devices, body(): moment, mass = lax.psum((moment_here, mass_here), 'items')  164 us
    pmax x2, blocking collectives, body(): top = lax.pmax(jnp.max(score, axis=1), 'cents')  47.4 us
    all_gather x2, blocking collectives, body(): total = jnp.sum(lax.all_gather(jnp.sum(expo, axis=1), 'cents'), axis=0)  36.5 us
    unnamed x1, blocking collectives  25.5 us
    gather x1, local copies, waits for them, and re-layouts, settle_rows(): return jnp.take(joined, source, axis=0)  10.8 us
  transfers between devices with their start and end apart: 4, of which 2 were waited for; matrix products, arithmetic and copies ran while one was open for 1% of the time, Pallas kernels for 0%

profile of v1, /device:TPU:64, one launch (start us, length us, event | category | flops | bytes accessed | tf_op | source)
XLA Modules:
  0.0 509.1 jit_solution(4997157799903163296)
XLA Ops:
  6.5 0.0 all-reduce.4.cloned.1.call-start
  7.2 1.3 constant_dynamic-slice_fusion.1
  8.5 3.5 collective-permute-start
  12.0 1.3 collective-permute-start.1
  13.3 1.3 dynamic-slice
  14.6 0.7 dynamic-update-slice
  15.4 25.5 %all-reduce = s32[32]{0:T(128)S(1)} all-reduce(s32[32]{0:T(128)S(1)} %dynamic-update-slice), channel_id=2, replica_groups=mesh['items'=32,'cents'=16] {'items'}, use_global_device_ids=true, to_apply=%add | all-reduce | flops 32 | bytes 256
  40.9 1.1 fusion.6
  42.0 0.0 collective-permute-done
  42.0 0.0 collective-permute-done.1
  42.0 3.9 pad_maximum_fusion
  46.0 0.0 copy-start
  46.0 10.8 %gather_fusion = bf16[1536,1024]{1,0:T(8,128)(2,1)} fusion(bf16[2304,1024]{1,0:T(8,128)(2,1)} %pad_maximum_fusion, s32[2048]{0:T(1024)S(1)} %pad_clamp_fusion), kind=kCustom, calls=%fused_computation | custom fusion | bytes 6297600 | tf_op jit(solution)/shard_map/jit(_take)/gather | solution.py:68
  56.7 0.0 copy-done
  56.7 3.2 fusion.18
  59.9 25.9 %pmax.14 = f32[1536]{0:T(1024)S(1)} all-reduce(f32[1536]{0:T(1024)S(1)} %get-tuple-element.45), channel_id=1, replica_groups=mesh['items'=32,'cents'=16] {'cents'}, use_global_device_ids=true, to_apply=%region_4.5 | all-reduce | flops 1536 | bytes 12288 | tf_op jit(solution)/shard_map/pmax | solution.py:82
  85.8 0.1 fusion.4
  85.9 17.9 %all-gather.3 = f32[16,1,1536]{2,1,0:T(1,128)S(1)} all-gather(f32[1,1,1536]{2,1,0:T(1,128)S(1)} %reshape.84), channel_id=3, replica_groups=mesh['items'=32,'cents'=16] {'cents'}, dimensions={0}, use_global_device_ids=true | all-gather | bytes 104448 | tf_op jit(solution)/shard_map/all_gather | solution.py:84
  103.8 0.1 reduce_sum.74
  103.9 0.2 convert_reduce_fusion.1
  104.1 3.4 fusion.16
  107.6 0.0 all-reduce.4.cloned.1.call-update
  107.6 0.0 all-reduce.6.cloned.1.call-start
  107.6 107.8 %psum.29 = f32[128]{0:T(128)S(1)} all-reduce(f32[128]{0:T(128)S(1)} %get-tuple-element.41), channel_id=1, replica_groups=mesh['items'=32,'cents'=16] {'items'}, use_global_device_ids=true, to_apply=%region_9.10 | all-reduce | flops 128 | bytes 1024 | tf_op jit(solution)/shard_map/psum | solution.py:90
  215.5 81.8 %all-reduce.4.cloned.1.call-done = f32[128,1024]{1,0:T(8,128)} async-done(((f32[128,1024]{1,0:T(8,128)}), f32[128,1024]{1,0:T(8,128)}) %all-reduce.4.cloned.1.call-update) | async-done | bytes 524304 | tf_op jit(solution)/shard_map/psum | solution.py:90
  297.3 1.3 fusion.10
  298.5 3.2 fusion.19
  301.7 21.5 %pmax.15 = f32[1536]{0:T(1024)S(1)} all-reduce(f32[1536]{0:T(1024)S(1)} %get-tuple-element.47), channel_id=1, replica_groups=mesh['items'=32,'cents'=16] {'cents'}, use_global_device_ids=true, to_apply=%region_12.13 | all-reduce | flops 1536 | bytes 12288 | tf_op jit(solution)/shard_map/pmax | solution.py:82
  323.2 0.1 fusion.5
  323.4 18.6 %all-gather.4 = f32[16,1,1536]{2,1,0:T(1,128)S(1)} all-gather(f32[1,1,1536]{2,1,0:T(1,128)S(1)} %reshape.86), channel_id=4, replica_groups=mesh['items'=32,'cents'=16] {'cents'}, dimensions={0}, use_global_device_ids=true | all-gather | bytes 104448 | tf_op jit(solution)/shard_map/all_gather | solution.py:84
  342.0 0.1 reduce_sum.78
  342.1 0.2 convert_reduce_fusion
  342.3 3.4 fusion.15
  345.7 0.0 all-reduce.6.cloned.1.call-update
  345.8 72.5 %psum.31 = f32[128]{0:T(128)S(1)} all-reduce(f32[128]{0:T(128)S(1)} %get-tuple-element.37), channel_id=1, replica_groups=mesh['items'=32,'cents'=16] {'items'}, use_global_device_ids=true, to_apply=%region_17.18 | all-reduce | flops 128 | bytes 1024 | tf_op jit(solution)/shard_map/psum | solution.py:90
  418.2 82.2 %all-reduce.6.cloned.1.call-done = f32[128,1024]{1,0:T(8,128)} async-done(((f32[128,1024]{1,0:T(8,128)}), f32[128,1024]{1,0:T(8,128)}) %all-reduce.6.cloned.1.call-update) | async-done | bytes 524304 | tf_op jit(solution)/shard_map/psum | solution.py:90
  500.5 1.9 fusion.13
  (9 shorter events, 0.1 us)
Async XLA Ops:
  6.5 290.8 %all-reduce.4.cloned.1.call-start = ((), (), s32[]{:S(2)}) async-start(), calls=%async_computation | async-start | bytes 1048576 | tf_op jit(solution)/shard_map/psum | solution.py:90
  8.5 33.6 %collective-permute-start = (bf16[192,1024]{1,0:T(8,128)(2,1)S(1)}, bf16[192,1024]{1,0:T(8,128)(2,1)S(1)}, u32[]{:S(2)}, u32[]{:S(2)}) collective-permute-start(bf16[192,1024]{1,0:T(8,128)(2,1)S(1)} %get-tuple-element.43), channel_id=1, source_target_pairs={{0,16},{16,32},{32,48},{48,64},{64,80},{80,96},{96,112},{112,128},... | collective-permute-start | bytes 1179656 | tf_op jit(solution)/shard_map/ppermute | solution.py:29
  12.0 30.1 %collective-permute-start.1 = (bf16[192,1024]{1,0:T(8,128)(2,1)S(1)}, bf16[192,1024]{1,0:T(8,128)(2,1)S(1)}, u32[]{:S(2)}, u32[]{:S(2)}) collective-permute-start(bf16[192,1024]{1,0:T(8,128)(2,1)S(1)} %get-tuple-element.44), channel_id=1, source_target_pairs={{16,0},{32,16},{48,32},{64,48},{80,64},{96,80},{112,96},{128,112},... | collective-permute-start | bytes 1179656 | tf_op jit(solution)/shard_map/ppermute | solution.py:32
  46.0 10.8 %copy-start = (bf16[128,1024]{1,0:T(8,128)(2,1)S(1)}, bf16[128,1024]{1,0:T(8,128)(2,1)}, u32[]{:S(2)}) copy-start(bf16[128,1024]{1,0:T(8,128)(2,1)} %param.7) | copy-start | bytes 786436
  107.6 392.9 %all-reduce.6.cloned.1.call-start = ((), (), s32[]{:S(2)}) async-start(), calls=%async_computation.1 | async-start | bytes 1048576 | tf_op jit(solution)/shard_map/psum | solution.py:90
Sparse Core Ops, SparseCore 0:
  107.7 189.5 all-reduce.3
  345.9 154.5 all-reduce.5
